TPU v7x, 128 devices: a whole 4x4x4 slice. The times are simulated.
128 devices in a mesh: dp: 8 (over x_lo, y), expert: 16 (over x_hi, z, core).
Axes of the slice: x: 4 (x_hi: 2, x_lo: 2; x = x_hi * 2 + x_lo), y: 4, z: 4, core: 2. Of those that a mesh axis runs over, the one named last changes fastest.
Arguments:
- tokens: bfloat16 [65536, 2048], P(('dp', 'expert')), may hold values from -6 to 6
- probe: bfloat16 [65536, 2048], P(('dp', 'expert')), may hold values from -20 to 20
- domain: int32 [65536], P(('dp', 'expert')), may hold values from 0 to 21
- mix: float32 [22], replicated, may hold values from 0.5 to 2
- router: bfloat16 [2048, 32], replicated, may hold values from -0.125 to 0.125
- picks: int32 [128, 32, 40], P(('dp', 'expert')), may hold values from 0 to 511, as said below
- w_gate: bfloat16 [2048, 32, 768], P(None, 'expert'), may hold values from -0.125 to 0.125
- w_up: bfloat16 [2048, 32, 768], P(None, 'expert'), may hold values from -0.125 to 0.125
- w_down: bfloat16 [2048, 32, 768], P(None, 'expert'), may hold values from -0.21875 to 0.21875
Outputs:
- domain_loss: float32 [22], replicated
- router_grad: float32 [2048, 32], replicated
- grad_gate: bfloat16 [2048, 32, 768], P('dp', 'expert')
- grad_up: bfloat16 [2048, 32, 768], P('dp', 'expert')
- grad_down: bfloat16 [2048, 32, 768], P('dp', 'expert')
Inputs may be any that keep to these rules, and one draw needn't show every extreme that they name: The 40 picks of one expert on one device are distinct token positions of that device.
All inputs are finite; a program needn't handle non-finite values.
Results may differ from a plain program's by a relative error of at most 0.018.
Values may be sent and summed in bfloat16 or wider, within the bound.
A program may use at most 192 MiB of HBM per device.

v0:
```python
import math

import jax
import jax.numpy as jnp
from jax import lax
from jax.sharding import PartitionSpec as P


def body(tokens, probe, domain, mix, router, picks, w_gate, w_up, w_down):
    token_count, model_width = tokens.shape
    expert_count = router.shape[1]
    slot_count = picks.shape[2]
    domain_count = mix.shape[0]
    data_devices = lax.axis_size("dp")
    expert_devices = lax.axis_size("expert")
    chosen = picks[0]
    logits = jnp.dot(tokens, router, preferred_element_type=jnp.float32)
    gate_vals = jax.nn.sigmoid(jnp.take_along_axis(logits.T, chosen, axis=1))
    outgoing = tokens[chosen].reshape(expert_count, 1, slot_count, model_width)
    received = lax.all_to_all(outgoing, "expert", split_axis=0, concat_axis=1, tiled=True)
    pre_gate = jnp.einsum("jsrd,djf->jsrf", received, w_gate, preferred_element_type=jnp.float32)
    pre_up = jnp.einsum("jsrd,djf->jsrf", received, w_up, preferred_element_type=jnp.float32)
    expert_hidden = (jax.nn.silu(pre_gate) * pre_up).astype(jnp.bfloat16)
    result = jnp.einsum(
        "jsrf,djf->jsrd", expert_hidden, w_down, preferred_element_type=jnp.float32
    ).astype(jnp.bfloat16)
    returned = lax.all_to_all(result, "expert", split_axis=1, concat_axis=0, tiled=True)
    returned, arrived, pre_gate, pre_up, hidden = (
        returned,
        received,
        pre_gate,
        pre_up,
        expert_hidden,
    )
    outputs = returned.reshape(expert_count, slot_count, model_width).astype(jnp.float32)
    contrib = gate_vals[:, :, None] * outputs
    flat_index = chosen.reshape(-1)
    added = (
        jnp.zeros((token_count, model_width), jnp.float32)
        .at[flat_index]
        .add(contrib.reshape(-1, model_width))
    )
    layer_out = tokens.astype(jnp.float32) + added
    difference = layer_out - probe.astype(jnp.float32)
    per_token = jnp.sum(difference * difference, axis=1)
    member = (domain[:, None] == jnp.arange(domain_count, dtype=jnp.int32)[None, :]).astype(
        jnp.float32
    )
    local_loss = jnp.sum(per_token[:, None] * member, axis=0)
    loss_total = lax.psum(local_loss, ("dp", "expert"))
    total_tokens = token_count * data_devices * expert_devices
    loss_scale = 1.0 / math.sqrt(data_devices * expert_devices * slot_count)
    weight_tok = jnp.sum(member * mix[None, :], axis=1)
    upstream = (loss_scale * weight_tok)[:, None] * difference
    picked_up = upstream[chosen]
    gate_slope = jnp.sum(picked_up * outputs, axis=2)
    logit_grad = gate_slope * gate_vals * (1.0 - gate_vals)
    expert_ids = jnp.broadcast_to(jnp.arange(expert_count, dtype=jnp.int32)[:, None], chosen.shape)
    placed = (
        jnp.zeros((token_count, expert_count), jnp.float32).at[chosen, expert_ids].set(logit_grad)
    )
    router_part = jnp.dot(tokens.astype(jnp.float32).T, placed, precision=lax.Precision.HIGHEST)
    sending = (
        (gate_vals[:, :, None] * picked_up)
        .astype(jnp.bfloat16)
        .reshape(expert_count, 1, slot_count, model_width)
    )
    back_grad = lax.all_to_all(sending, "expert", split_axis=0, concat_axis=1, tiled=True)
    hidden_grad = jnp.einsum(
        "jsrd,djf->jsrf", back_grad, w_down, preferred_element_type=jnp.float32
    )
    sigmoid_gate = jax.nn.sigmoid(pre_gate)
    gate_in = (
        hidden_grad * pre_up * sigmoid_gate * (1.0 + pre_gate * (1.0 - sigmoid_gate))
    ).astype(jnp.bfloat16)
    up_in = (hidden_grad * jax.nn.silu(pre_gate)).astype(jnp.bfloat16)

    def input_term(grads_in):
        return jnp.einsum("jsrd,jsrf->djf", arrived, grads_in, preferred_element_type=jnp.float32)

    grad_gate = lax.psum_scatter(
        input_term(gate_in).astype(jnp.bfloat16), "dp", scatter_dimension=0, tiled=True
    )
    grad_up = lax.psum_scatter(
        input_term(up_in).astype(jnp.bfloat16), "dp", scatter_dimension=0, tiled=True
    )
    grad_down = lax.psum_scatter(
        jnp.einsum("jsrd,jsrf->djf", back_grad, hidden, preferred_element_type=jnp.float32).astype(
            jnp.bfloat16
        ),
        "dp",
        scatter_dimension=0,
        tiled=True,
    )
    router_total = lax.psum(router_part, ("dp", "expert"))
    domain_loss = loss_total * (domain_count / (total_tokens * model_width))
    return (domain_loss, router_total, grad_gate, grad_up, grad_down)


def solution(mesh):
    placed = (
        P(("dp", "expert"), None),
        P(("dp", "expert"), None),
        P(("dp", "expert")),
        P(),
        P(),
        P(("dp", "expert"), None, None),
        P(None, "expert", None),
        P(None, "expert", None),
        P(None, "expert", None),
    )
    return jax.shard_map(
        body,
        mesh=mesh,
        in_specs=placed,
        out_specs=(
            P(),
            P(),
            P("dp", "expert", None),
            P("dp", "expert", None),
            P("dp", "expert", None),
        ),
        check_vma=False,
    )
```

profile of v0, /device:TPU:1, one launch (start us, length us, event | category | flops | bytes accessed | tf_op | source)
XLA Modules:
  0.0 717.5 jit_solution(11860185707785233741)
XLA Ops:
  8.0 0.8 shift-left_or_fusion
  8.8 0.1 reshape.151
  8.9 12.7 %gather_fusion = bf16[1280,2048]{1,0:T(8,128)(2,1)} fusion(bf16[512,2048]{1,0:T(8,128)(2,1)} %param.9, s32[2048]{0:T(1024)S(1)} %pad_clamp_fusion), kind=kCustom, calls=%fused_computation | custom fusion | bytes 10490880 | tf_op jit(solution)/shard_map/gather | solution.py:19
  21.6 71.9 %all_to_all.45 = bf16[32,1,40,2048]{3,2,1,0:T(8,128)(2,1)S(1)} all-to-all(bf16[32,1,40,2048]{3,2,1,0:T(8,128)(2,1)} %bitcast.90), channel_id=1, replica_groups=mesh['dp'=8,'expert'=16] {'expert'}, dimensions={0} | all-to-all | bytes 10485760 | tf_op jit(solution)/shard_map/all_to_all | solution.py:20
  93.5 4.4 fusion.6
  97.9 6.5 multiply_convert_fusion.3
  104.5 7.7 %fusion.20 = bf16[2,16,40,2048]{3,2,1,0:T(8,128)(2,1)S(1)} fusion(bf16[2,16,40,768]{3,2,1,0:T(8,128)(2,1)} %get-tuple-element.36, bf16[2048,2,768,1]{2,1,0,3:T(2,128)(2,1)} %bitcast.102), kind=kOutput, calls=%fused_computation.34 | convolution fusion | flops 4029153280 | bytes 13500416 | tf_op jit(solution)/shard_map/jsrf,djf->jsrd/dot_general | solution.py:24
  112.2 2.7 copy.64
  114.9 5.6 all-to-all-start.1
  120.5 0.2 reduce-scatter.8.cloned.1.call-start
  120.8 0.1 squeeze.7
  120.9 2.5 convert_element_type.66
  123.4 0.1 reshape_squeeze.3
  123.5 0.1 reshape.165
  123.6 0.7 fusion.36
  124.3 10.1 %gather_fusion.2 = f32[1280]{0:T(1024)S(1)} fusion(f32[32,512]{1,0:T(8,128)S(1)} %fusion.36, s32[1280]{0:T(1024)S(1)} %reshape.165), kind=kCustom, calls=%fused_computation.2 | custom fusion | bytes 20480 | tf_op jit(solution)/shard_map/jit(take_along_axis)/gather | solution.py:18
  134.6 55.3 %all-to-all-done.1 = bf16[2,16,40,2048]{3,2,0,1:T(8,128)(2,1)} async-done(((bf16[2,16,40,2048]{3,2,0,1:T(8,128)(2,1)}), bf16[2,16,40,2048]{3,2,0,1:T(8,128)(2,1)}, u32[]{:S(2)}, u32[]{:S(2)}) %all-to-all-start.1) | async-done | bytes 5242912 | tf_op jit(solution)/shard_map/all_to_all | solution.py:27
  189.9 3.9 bitcast_convert_fusion.3
  193.8 4.6 bitcast_multiply_fusion
  198.4 25.4 %scatter_fusion = f32[512,2048]{1,0:T(8,128)} fusion(f32[512,2048]{1,0:T(8,128)} %convert_element_type.66, s32[1280]{0:T(1024)S(1)} %fusion.33, f32[1280,2048]{1,0:T(8,128)} %bitcast_multiply_fusion), kind=kCustom, calls=%fused_computation.3 | custom fusion | flops 2621440 | bytes 31462400 | tf_op jit(solution)/shard_map/scatter-add | solution.py:41
  223.8 3.0 multiply_reduce_fusion
  226.8 0.1 select_reduce_fusion
  226.9 0.3 copy-done.2
  227.3 2.5 fusion.28
  229.8 13.0 %gather_fusion.1 = f32[1280,2048]{1,0:T(8,128)} fusion(f32[512,2048]{1,0:T(8,128)} %fusion.28, s32[2048]{0:T(1024)S(1)} %pad_clamp_fusion), kind=kCustom, calls=%fused_computation.1 | custom fusion | bytes 20976640 | tf_op jit(solution)/shard_map/gather | solution.py:55
  242.8 6.7 fusion
  249.6 1.7 copy-done.5
  251.3 2.9 multiply_convert_fusion
  254.1 76.7 %all_to_all.46 = bf16[32,1,40,2048]{3,2,1,0:T(8,128)(2,1)S(1)} all-to-all(bf16[32,1,40,2048]{3,2,1,0:T(8,128)(2,1)} %multiply_convert_fusion), channel_id=1, replica_groups=mesh['dp'=8,'expert'=16] {'expert'}, dimensions={0} | all-to-all | bytes 10485760 | tf_op jit(solution)/shard_map/all_to_all | solution.py:68
  330.8 2.3 copy-done.8
  333.1 7.1 fusion.3
  340.2 0.3 reduce-scatter.6.cloned.1.call-start
  340.5 8.2 %fusion.8 = f32[2,16,40,768]{3,2,1,0:T(8,128)S(1)} fusion(bf16[2048,2,768,1]{2,1,0,3:T(2,128)(2,1)} %bitcast.103, bf16[16,2,1,40,2048]{4,3,1,0,2:T(8,128)(2,1)} %bitcast.96), kind=kOutput, calls=%fused_computation.19 | convolution fusion | flops 4026531840 | bytes 15466496 | tf_op jit(solution)/shard_map/jsrd,djf->jsrf/dot_general | solution.py:69
  348.7 1.9 copy-done.19
  350.7 9.9 %fusion.2 = bf16[2048,2,768]{0,2,1:T(8,128)(2,1)} fusion(bf16[16,2,1,40,2048]{4,3,1,0,2:T(8,128)(2,1)} %bitcast.93, f32[2,16,40,768]{3,2,1,0:T(8,128)S(1)} %fusion.8, f32[2,16,40,768]{3,2,1,0:T(8,128)S(1)} %copy-done.18), kind=kOutput, calls=%fused_computation.13 | convolution fusion | flops 4035575808 | bytes 19398656 | tf_op jit(solution)/shard_map/jsrd,jsrf->djf/dot_general | solution.py:79
  360.6 12.5 %fusion.1 = bf16[2048,2,768]{0,2,1:T(8,128)(2,1)} fusion(bf16[16,2,1,40,2048]{4,3,1,0,2:T(8,128)(2,1)} %bitcast.94, f32[2,16,40,768]{3,2,1,0:T(8,128)} %copy-done.17, f32[2,16,40,768]{3,2,1,0:T(8,128)} %copy-done.19, f32[2,16,40,768]{3,2,1,0:T(8,128)} %get-tuple-element.37), kind=kOutput, calls=%fused_computation.12 | convolution fusion | flops 4039507968 | bytes 23330816 | tf_op jit(solution)/shard_map/jsrd,jsrf->djf/dot_general | solution.py:79
  373.2 0.6 copy-done.11
  374.0 0.1 reshape.179
  374.1 187.1 %psum.14 = f32[22]{0:T(128)S(1)} all-reduce(f32[22]{0:T(128)S(1)} %get-tuple-element.31), channel_id=1, replica_groups=mesh['dp'=8,'expert'=16] {'dp','expert'}, use_global_device_ids=true, to_apply=%region_3.4 | all-reduce | flops 22 | bytes 176 | tf_op jit(solution)/shard_map/psum | solution.py:50
  561.2 0.1 reshape.181
  561.3 5.3 scatter_custom_fusion.1
  566.6 1.8 convolution_bitcast_fusion
  568.5 0.5 broadcast_multiply_fusion.1
  569.0 3.0 copy.72
  572.0 3.0 copy.71
  575.1 3.0 copy.70
  578.1 130.3 %all-reduce.2.cloned.1.call-done = f32[2048,32]{0,1:T(8,128)} async-done(((f32[2048,32]{0,1:T(8,128)}), f32[2048,32]{0,1:T(8,128)}) %all-reduce.2.cloned.1.call-update) | async-done | bytes 262160 | tf_op jit(solution)/shard_map/psum | solution.py:95
  708.4 1.7 copy.129
  (62 shorter events, 0.6 us)
Async XLA Ops:
  8.0 115.6 %copy-start = (bf16[2048,32]{0,1:T(8,128)(2,1)S(1)}, bf16[2048,32]{0,1:T(8,128)(2,1)}, u32[]{:S(2)}) copy-start(bf16[2048,32]{0,1:T(8,128)(2,1)} %param.13) | copy-start | bytes 393220
  8.8 12.8 %copy-start.10 = (s32[32,40,1]{1,0,2:T(8,128)}, s32[32,40,1]{1,0,2:T(8,128)S(1)}, u32[]{:S(2)}) copy-start(s32[32,40,1]{1,0,2:T(8,128)S(1)} %get-tuple-element.35) | copy-start | bytes 15364
  21.6 71.9 %copy-start.16 = (bf16[2048,2,768]{2,1,0:T(2,128)(2,1)S(1)}, bf16[2048,2,768]{2,1,0:T(2,128)(2,1)}, u32[]{:S(2)}) copy-start(bf16[2048,2,768]{2,1,0:T(2,128)(2,1)} %param.15) | copy-start | bytes 18874372
  21.6 76.3 %slice-start = ((s8[6291456]{0:T(1024)(128)(4,1)}), s8[4194304]{0:T(1024)(128)(4,1)S(1)}, s32[]{:S(2)}) async-start(s8[6291456]{0:T(1024)(128)(4,1)} %bitcast.99), calls=%async_computation.10 | async-start | bytes 8388608
  93.5 4.4 copy-start.7
  93.5 4.4 slice-start.1
  97.9 6.6 copy-start.17
  114.9 5.8 copy-start.9
  114.9 5.9 copy-start.3
  114.9 75.0 %all-to-all-start.1 = ((bf16[2,16,40,2048]{3,2,0,1:T(8,128)(2,1)}), bf16[2,16,40,2048]{3,2,0,1:T(8,128)(2,1)}, u32[]{:S(2)}, u32[]{:S(2)}) async-start(bf16[2,16,40,2048]{3,2,0,1:T(8,128)(2,1)} %copy.64), calls=%async_computation.1 | async-start | bytes 10485760 | tf_op jit(solution)/shard_map/all_to_all | solution.py:27
  120.5 448.4 %reduce-scatter.8.cloned.1.call-start = ((), (), s32[]{:S(2)}) async-start(), calls=%async_computation.9 | async-start | bytes 7077888 | tf_op jit(solution)/shard_map/reduce_scatter | solution.py:87
  198.4 25.4 %copy-start.6 = (bf16[512,2048]{1,0:T(8,128)(2,1)S(1)}, bf16[512,2048]{1,0:T(8,128)(2,1)}, u32[]{:S(2)}) copy-start(bf16[512,2048]{1,0:T(8,128)(2,1)} %param.10) | copy-start | bytes 6291460
  223.8 3.0 copy-start.12
  223.8 3.0 copy-start.15
  223.8 3.5 copy-start.2
  242.8 8.5 %copy-start.5 = (f32[1280,2048]{1,0:T(8,128)S(1)}, f32[1280,2048]{1,0:T(8,128)}, u32[]{:S(2)}) copy-start(f32[1280,2048]{1,0:T(8,128)} %gather_fusion.1) | copy-start | bytes 31457284
  254.1 79.0 %copy-start.20 = (bf16[2,16,40,768]{3,2,1,0:T(8,128)(2,1)S(1)}, bf16[2,16,40,768]{3,2,1,0:T(8,128)(2,1)}, u32[]{:S(2)}) copy-start(bf16[2,16,40,768]{3,2,1,0:T(8,128)(2,1)} %get-tuple-element.36) | copy-start | bytes 5898244
  330.8 2.3 copy-start.8
  340.2 231.8 %reduce-scatter.6.cloned.1.call-start = ((), (), s32[]{:S(2)}) async-start(), calls=%async_computation.8 | async-start | bytes 7077888 | tf_op jit(solution)/shard_map/reduce_scatter | solution.py:84
  340.5 10.1 %copy-start.18 = (f32[2,16,40,768]{3,2,1,0:T(8,128)S(1)}, f32[2,16,40,768]{3,2,1,0:T(8,128)}, u32[]{:S(2)}) copy-start(f32[2,16,40,768]{3,2,1,0:T(8,128)} %copy-done.17) | copy-start | bytes 11796484
  348.7 1.9 copy-start.19
  360.6 214.5 %reduce-scatter.4.cloned.1.call-start = ((), (), s32[]{:S(2)}) async-start(), calls=%async_computation.7 | async-start | bytes 7077888 | tf_op jit(solution)/shard_map/reduce_scatter | solution.py:81
  373.1 0.7 copy-start.11
  373.1 0.7 copy-start.13
  373.1 0.8 copy-start.14
  373.1 193.5 %copy-start.4 = (bf16[512,2048]{1,0:T(8,128)(2,1)S(1)}, bf16[512,2048]{1,0:T(8,128)(2,1)}, u32[]{:S(2)}) copy-start(bf16[512,2048]{1,0:T(8,128)(2,1)} %param.9) | copy-start | bytes 6291460
  373.1 336.9 %copy-start.1 = (bf16[2048,32]{0,1:T(8,128)(2,1)S(1)}, bf16[2048,32]{0,1:T(8,128)(2,1)}, u32[]{:S(2)}) copy-start(bf16[2048,32]{0,1:T(8,128)(2,1)} %param.13) | copy-start | bytes 393220
  373.2 335.2 %all-reduce.2.cloned.1.call-start = ((), (), s32[]{:S(2)}) async-start(), calls=%async_computation.6 | async-start | bytes 524288 | tf_op jit(solution)/shard_map/psum | solution.py:95
Sparse Core Ops, SparseCore 0:
  340.3 71.2 reduce-scatter.7
  414.1 71.8 reduce-scatter.5
  488.3 72.0 reduce-scatter.3
Sparse Core Ops, SparseCore 1:
  568.6 139.8 all-reduce.1
where the time goes:
time: 720 us; the launch traced here: 717 us
  blocking collectives  336 us (47%)
  waiting for transfers between devices  186 us (26%)
  local copies, waits for them, and re-layouts  62.2 us (9%)
  matrix products  58.8 us (8%)
  other arithmetic  53.1 us (7%)
  between operations  15.8 us (2%)
    psum x1, blocking collectives, body(): loss_total = lax.psum(local_loss, ('dp', 'expert'))  187 us
    psum x1, waiting for transfers between devices, body(): router_total = lax.psum(router_part, ('dp', 'expert'))  130 us
    all_to_all x1, blocking collectives, body(): lax.all_to_all(sending, 'expert', split_axis=0, concat_axis=1, tiled=True)  76.7 us
    all_to_all x1, blocking collectives, body(): lax.all_to_all(outgoing, 'expert', split_axis=0, concat_axis=1, tiled=True)  71.9 us
    all_to_all x1, waiting for transfers between devices, body(): lax.all_to_all(result, 'expert', split_axis=1, concat_axis=0, tiled=True)  55.3 us
    scatter-add x1, other arithmetic, body(): added = jnp.zeros((token_count, model_width), jnp.float32).at[flat_index]...  25.4 us
    unnamed x53, local copies, waits for them, and re-layouts  23.1 us
    dot_general x2, matrix products, input_term(): jnp.einsum('jsrd,jsrf->djf', arrived, grads_in, preferred_element_type=jn...  22.3 us
  transfers between devices with their start and end apart: 5, of which 2 were waited for; matrix products, arithmetic and copies ran while one was open for 9% of the time, Pallas kernels for 0%

commit v1 on v0

v1 whole, which is shorter than its diff:
```python
import math

import jax
import jax.numpy as jnp
from jax import lax
from jax.sharding import PartitionSpec as P

BF = jnp.bfloat16
F32 = jnp.float32


def body(tokens, probe, domain, mix, router, picks, w_gate, w_up, w_down):
    token_count, model_width = tokens.shape
    expert_count = router.shape[1]
    slot_count = picks.shape[2]
    pick_count = expert_count * slot_count
    domain_count = mix.shape[0]
    device_count = lax.axis_size("dp") * lax.axis_size("expert")
    flat = picks[0].reshape(pick_count)
    token_ids = jnp.arange(token_count, dtype=jnp.int32)
    select = (flat[:, None] == token_ids[None, :]).astype(BF)
    expert_of = jnp.repeat(jnp.arange(expert_count, dtype=jnp.int32), slot_count)
    own_expert = expert_of[:, None] == jnp.arange(expert_count, dtype=jnp.int32)[None, :]
    outgoing = jnp.dot(select, tokens, preferred_element_type=F32).astype(BF)
    received = lax.all_to_all(
        outgoing.reshape(expert_count, 1, slot_count, model_width),
        "expert", split_axis=0, concat_axis=1, tiled=True,
    )
    logits = jnp.dot(outgoing, router, preferred_element_type=F32)
    gate = jax.nn.sigmoid(jnp.sum(jnp.where(own_expert, logits, 0.0), axis=1))
    pre_gate = jnp.einsum("jsrd,djf->jsrf", received, w_gate, preferred_element_type=F32)
    pre_up = jnp.einsum("jsrd,djf->jsrf", received, w_up, preferred_element_type=F32)
    hidden = (jax.nn.silu(pre_gate) * pre_up).astype(BF)
    result = jnp.einsum("jsrf,djf->jsrd", hidden, w_down, preferred_element_type=F32).astype(BF)
    returned = lax.all_to_all(result, "expert", split_axis=1, concat_axis=0, tiled=True)
    returned = returned.reshape(pick_count, model_width)
    weighted = jnp.where(
        flat[None, :] == token_ids[:, None], gate.astype(BF)[None, :], jnp.zeros((), BF)
    )
    added = jnp.dot(weighted, returned, preferred_element_type=F32)
    difference = tokens.astype(F32) + added - probe.astype(F32)
    per_token = jnp.sum(difference * difference, axis=1)
    member = (domain[:, None] == jnp.arange(domain_count, dtype=jnp.int32)[None, :]).astype(F32)
    local_loss = jnp.sum(per_token[:, None] * member, axis=0)
    loss_scale = 1.0 / math.sqrt(device_count * slot_count)
    weight_tok = jnp.sum(member * mix[None, :], axis=1)
    upstream = ((loss_scale * weight_tok)[:, None] * difference).astype(BF)
    picked_up = jnp.dot(select, upstream, preferred_element_type=F32)
    sending = (gate[:, None] * picked_up).astype(BF)
    gate_slope = jnp.sum(picked_up * returned.astype(F32), axis=1)
    logit_grad = gate_slope * gate * (1.0 - gate)
    placing = jnp.where(own_expert, logit_grad[:, None], 0.0)
    high = placing.astype(BF)
    low = (placing - high.astype(F32)).astype(BF)
    placed = lax.dot_general(
        select, jnp.concatenate([high, low], axis=1), (((0,), (0,)), ((), ())),
        preferred_element_type=F32,
    ).astype(BF)
    router_part = lax.dot_general(
        tokens, placed, (((0,), (0,)), ((), ())), preferred_element_type=F32
    )
    router_part = router_part[:, :expert_count] + router_part[:, expert_count:]
    loss_rows = jnp.zeros((8, expert_count), F32).at[0, :domain_count].set(local_loss)
    summed = lax.psum(jnp.concatenate([router_part, loss_rows], axis=0), ("dp", "expert"))
    back_grad = lax.all_to_all(
        sending.reshape(expert_count, 1, slot_count, model_width),
        "expert", split_axis=0, concat_axis=1, tiled=True,
    )

    def reduced(left, right):
        part = jnp.einsum("jsrd,jsrf->djf", left, right, preferred_element_type=F32)
        return lax.psum_scatter(part.astype(BF), "dp", scatter_dimension=0, tiled=True)

    grad_down = reduced(back_grad, hidden)
    hidden_grad = jnp.einsum("jsrd,djf->jsrf", back_grad, w_down, preferred_element_type=F32)
    sigmoid_gate = jax.nn.sigmoid(pre_gate)
    gate_in = (
        hidden_grad * pre_up * sigmoid_gate * (1.0 + pre_gate * (1.0 - sigmoid_gate))
    ).astype(BF)
    up_in = (hidden_grad * (pre_gate * sigmoid_gate)).astype(BF)
    grad_gate = reduced(received, gate_in)
    grad_up = reduced(received, up_in)
    domain_loss = summed[model_width, :domain_count] * (
        domain_count / (token_count * device_count * model_width)
    )
    return (domain_loss, summed[:model_width], grad_gate, grad_up, grad_down)


def solution(mesh):
    placed = (
        P(("dp", "expert"), None),
        P(("dp", "expert"), None),
        P(("dp", "expert")),
        P(),
        P(),
        P(("dp", "expert"), None, None),
        P(None, "expert", None),
        P(None, "expert", None),
        P(None, "expert", None),
    )
    return jax.shard_map(
        body,
        mesh=mesh,
        in_specs=placed,
        out_specs=(
            P(),
            P(),
            P("dp", "expert", None),
            P("dp", "expert", None),
            P("dp", "expert", None),
        ),
        check_vma=False,
    )
```

time: 720 us -> 531 us (0.74)
  blocking collectives: 336 us -> 71.2 us
  waiting for transfers between devices: 186 us -> 321 us
  other arithmetic: 53.1 us -> 2.29 us
  local copies, waits for them, and re-layouts: 62.2 us -> 16.6 us
  matrix products: 58.8 us -> 82.8 us
  starting transfers between devices: 6.21 us -> 20.8 us
    psum x1 -> x0, blocking collectives: 187 us -> none  [body(): loss_total = lax.psum(local_loss, ('dp', 'expert'))]
    all_to_all x2 -> x1, blocking collectives: 149 us -> 71.2 us  [body(): lax.all_to_all(outgoing.reshape(expert_count, 1, slot_count, model_width)...]
    all_to_all x0 -> x1, waiting for transfers between devices: none -> 68.4 us  [body(): lax.all_to_all(sending.reshape(expert_count, 1, slot_count, model_width),...]
    reduce_scatter x3, waiting for transfers between devices: 0.01 us -> 58.3 us  [reduced(): lax.psum_scatter(part.astype(BF), 'dp', scatter_dimension=0, tiled=True)]
    gather x5 -> x0, local copies, waits for them, and re-layouts: 36 us -> none  [the longest x1 13 us: body(): picked_up = upstream[chosen]]
    scatter-add x1 -> x0, other arithmetic: 25.4 us -> none  [body(): added = jnp.zeros((token_count, model_width), jnp.float32).at[flat_index]...]
    dot_general x9 -> x12, matrix products: 58.8 us -> 82.8 us  [the longest x3 32 us: reduced(): part = jnp.einsum('jsrd,jsrf->djf', left, right, preferred_element_type=F32)]
    all_to_all x0 -> x1, starting transfers between devices: none -> 14.7 us  [body(): lax.all_to_all(sending.reshape(expert_count, 1, slot_count, model_width),...]
  transfers between devices with their start and end apart: 5 -> 6, of which waited for: 2 -> 4; matrix products, arithmetic and copies ran while one was open for 9% -> 10% of each run, Pallas kernels for 0% -> 0%
where the time goes in v1:
time: 531 us
  waiting for transfers between devices  321 us (60%)
  matrix products  82.8 us (16%)
  blocking collectives  71.2 us (13%)
  starting transfers between devices  20.8 us (4%)
  local copies, waits for them, and re-layouts  16.6 us (3%)
  between operations  15.9 us (3%)
    psum x1, waiting for transfers between devices, body(): lax.psum(jnp.concatenate([router_part, loss_rows], axis=0), ('dp', 'exper...  130 us
    all_to_all x1, blocking collectives, body(): lax.all_to_all(outgoing.reshape(expert_count, 1, slot_count, model_width)...  71.2 us
    all_to_all x1, waiting for transfers between devices, body(): lax.all_to_all(sending.reshape(expert_count, 1, slot_count, model_width),...  68.4 us
    all_to_all x1, waiting for transfers between devices, body(): lax.all_to_all(result, 'expert', split_axis=1, concat_axis=0, tiled=True)  64.9 us
    reduce_scatter x3, waiting for transfers between devices, reduced(): lax.psum_scatter(part.astype(BF), 'dp', scatter_dimension=0, tiled=True)  58.3 us
    dot_general x3, matrix products, reduced(): part = jnp.einsum('jsrd,jsrf->djf', left, right, preferred_element_type=F32)  32 us
    all_to_all x1, starting transfers between devices, body(): lax.all_to_all(sending.reshape(expert_count, 1, slot_count, model_width),...  14.7 us
    unnamed x29, local copies, waits for them, and re-layouts  11.1 us
  transfers between devices with their start and end apart: 6, of which 4 were waited for; matrix products, arithmetic and copies ran while one was open for 10% of the time, Pallas kernels for 0%

profile of v1, /device:TPU:1, one launch (start us, length us, event | category | flops | bytes accessed | tf_op | source)
XLA Modules:
  0.0 530.8 jit_solution(12913081817586084446)
XLA Ops:
  8.0 0.0 copy-start
  8.0 0.8 eq.64
  8.9 4.9 convolution_convert_fusion
  13.8 0.0 copy-start.7
  13.8 0.0 slice-start
  13.8 71.2 %all_to_all.51 = bf16[32,1,40,2048]{3,2,1,0:T(8,128)(2,1)S(1)} all-to-all(bf16[32,1,40,2048]{3,2,1,0:T(8,128)(2,1)S(1)} %bitcast.69), channel_id=1, replica_groups=mesh['dp'=8,'expert'=16] {'expert'}, dimensions={0} | all-to-all | bytes 10485760 | tf_op jit(solution)/shard_map/all_to_all | solution.py:25
  85.0 4.4 fusion.5
  89.4 0.0 copy-start.8
  89.4 0.0 copy-done.3
  89.4 0.0 slice-done
  89.4 0.0 slice-done.1
  89.4 6.5 %multiply_convert_fusion.4 = (bf16[2,16,40,768]{3,2,1,0:T(8,128)(2,1)}, f32[2,16,40,768]{3,2,1,0:T(8,128)}) fusion(f32[2,16,40,768]{3,2,1,0:T(8,128)S(1)} %fusion.5, bf16[2048,2,768,1]{2,1,0,3:T(2,128)(2,1)S(1)} %bitcast.79, bf16[16,2,1,40,2048]{4,3,1,0,2:T(8,128)(2,1)S(1)} %bitcast.71), kind=kOutput, calls=%fused_computation.31 | convolution fusion | flops 4032430080 | bytes 21364736 | tf_op jit(solution)/shard_map/jsrd,djf->jsrf/dot_general | solution.py:32
  96.0 7.7 %fusion.19 = bf16[2,16,40,2048]{3,2,1,0:T(8,128)(2,1)S(1)} fusion(bf16[2,16,40,768]{3,2,1,0:T(8,128)(2,1)} %get-tuple-element.43, bf16[2048,2,768,1]{2,1,0,3:T(2,128)(2,1)} %bitcast.80), kind=kOutput, calls=%fused_computation.28 | convolution fusion | flops 4029153280 | bytes 13500416 | tf_op jit(solution)/shard_map/jsrf,djf->jsrd/dot_general | solution.py:34
  103.6 2.8 copy.51
  106.4 5.7 %all-to-all-start.1 = ((bf16[2,16,40,2048]{3,2,0,1:T(8,128)(2,1)}), bf16[2,16,40,2048]{3,2,0,1:T(8,128)(2,1)}, u32[]{:S(2)}, u32[]{:S(2)}) async-start(bf16[2,16,40,2048]{3,2,0,1:T(8,128)(2,1)} %copy.51), calls=%async_computation.1 | async-start | bytes 10485760 | tf_op jit(solution)/shard_map/all_to_all | solution.py:35
  112.2 0.1 eq.68
  112.2 4.3 fusion.38
  116.6 64.9 %all-to-all-done.1 = bf16[2,16,40,2048]{3,2,0,1:T(8,128)(2,1)} async-done(((bf16[2,16,40,2048]{3,2,0,1:T(8,128)(2,1)}), bf16[2,16,40,2048]{3,2,0,1:T(8,128)(2,1)}, u32[]{:S(2)}, u32[]{:S(2)}) %all-to-all-start.1) | async-done | bytes 5242912 | tf_op jit(solution)/shard_map/all_to_all | solution.py:35
  181.5 6.5 %multiply_reduce_fusion.1 = (f32[512]{0:T(512)S(1)}, f32[512,2048]{1,0:T(8,128)S(1)}) fusion(bf16[512,2048]{1,0:T(8,128)(2,1)} %param.12, bf16[1280,2048]{1,0:T(8,128)(2,1)} %bitcast.11, s32[1280]{0:T(1024)S(1)} %eq.64, bf16[1280]{0:T(1024)(128)(2,1)S(1)} %get-tuple-element.42, bf16[512,2048]{1,0:T(8,128)(2,1)S(1)} %copy-done.4), kind=kOutput, calls=%fused_computation.25 | convolution fusion | flops 2691956224 | bytes 13641216 | tf_op jit(solution)/shard_map/dot_general | solution.py:40
  188.0 0.1 select_reduce_fusion.1
  188.1 7.4 %multiply_convert_fusion = (bf16[1280,2048]{1,0:T(8,128)(2,1)}, f32[1280]{0:T(1024)S(1)}) fusion(f32[1280]{0:T(1024)S(1)} %get-tuple-element.41, bf16[2,16,40,2048]{3,2,0,1:T(8,128)(2,1)} %all-to-all-done.1, f32[512,2048]{1,0:T(8,128)S(1)} %get-tuple-element.46, f32[512]{0:T(512)S(1)} %broadcast_multiply_fusion, s32[1280]{0:T(1024)S(1)} %eq.64), kind=kOutput, calls=%fused_computation.3 | convolution fusion | flops 2700212992 | bytes 14697472 | tf_op jit(solution)/shard_map/dot_general | solution.py:48
  195.5 14.7 %all-to-all-start.2 = ((bf16[32,1,40,2048]{3,2,1,0:T(8,128)(2,1)}), bf16[32,1,40,2048]{3,2,1,0:T(8,128)(2,1)}, u32[]{:S(2)}, u32[]{:S(2)}) async-start(bf16[32,1,40,2048]{3,2,1,0:T(8,128)(2,1)} %bitcast.74), calls=%async_computation.2 | async-start | bytes 10485760 | tf_op jit(solution)/shard_map/all_to_all | solution.py:65
  210.2 0.0 all-reduce.3.cloned.1.call-start
  210.2 0.1 copy.52
  210.4 1.0 convolution_bitcast_fusion
  211.5 0.7 select_maximum_fusion
  212.2 0.0 all-reduce.3.cloned.1.call-update
  212.2 0.0 reduce-scatter.8.cloned.1.call-start
  212.3 68.4 %all-to-all-done.2 = bf16[32,1,40,2048]{3,2,1,0:T(8,128)(2,1)} async-done(((bf16[32,1,40,2048]{3,2,1,0:T(8,128)(2,1)}), bf16[32,1,40,2048]{3,2,1,0:T(8,128)(2,1)}, u32[]{:S(2)}, u32[]{:S(2)}) %all-to-all-start.2) | async-done | bytes 5242912 | tf_op jit(solution)/shard_map/all_to_all | solution.py:65
  280.7 9.8 %fusion.2 = bf16[2048,2,768]{0,2,1:T(8,128)(2,1)} fusion(bf16[2,16,40,768]{3,2,1,0:T(8,128)(2,1)} %get-tuple-element.43, bf16[16,2,1,40,2048]{4,3,1,0,2:T(8,128)(2,1)} %bitcast.18), kind=kOutput, calls=%fused_computation.8 | convolution fusion | flops 4029677568 | bytes 13500416 | tf_op jit(solution)/shard_map/jsrd,jsrf->djf/dot_general | solution.py:71
  290.5 0.0 reduce-scatter.8.cloned.1.call-update
  290.5 0.3 reduce-scatter.6.cloned.1.call-start
  290.8 8.2 %fusion.7 = f32[2,16,40,768]{3,2,1,0:T(8,128)S(1)} fusion(bf16[2048,2,768,1]{2,1,0,3:T(2,128)(2,1)} %bitcast.81, bf16[16,2,1,40,2048]{4,3,1,0,2:T(8,128)(2,1)} %bitcast.18), kind=kOutput, calls=%fused_computation.13 | convolution fusion | flops 4026531840 | bytes 15466496 | tf_op jit(solution)/shard_map/jsrd,djf->jsrf/dot_general | solution.py:75
  299.0 1.8 copy-done.10
  300.9 9.9 %fusion.1 = bf16[2048,2,768]{0,2,1:T(8,128)(2,1)} fusion(bf16[16,2,1,40,2048]{4,3,1,0,2:T(8,128)(2,1)} %bitcast.72, f32[2,16,40,768]{3,2,1,0:T(8,128)S(1)} %fusion.7, f32[2,16,40,768]{3,2,1,0:T(8,128)S(1)} %copy-done.9), kind=kOutput, calls=%fused_computation.7 | convolution fusion | flops 4035575808 | bytes 19398656 | tf_op jit(solution)/shard_map/jsrd,jsrf->djf/dot_general | solution.py:71
  310.8 0.0 reduce-scatter.6.cloned.1.call-update
  310.8 0.0 reduce-scatter.4.cloned.1.call-start
  310.8 12.3 %fusion = bf16[2048,2,768]{0,2,1:T(8,128)(2,1)} fusion(bf16[16,2,1,40,2048]{4,3,1,0,2:T(8,128)(2,1)} %bitcast.73, f32[2,16,40,768]{3,2,1,0:T(8,128)} %copy-done.8, f32[2,16,40,768]{3,2,1,0:T(8,128)} %copy-done.10, f32[2,16,40,768]{3,2,1,0:T(8,128)} %get-tuple-element.44), kind=kOutput, calls=%fused_computation.6 | convolution fusion | flops 4039507968 | bytes 23330816 | tf_op jit(solution)/shard_map/jsrd,jsrf->djf/dot_general | solution.py:71
  323.1 0.0 reduce-scatter.4.cloned.1.call-update
  323.1 0.0 copy-start.1
  323.2 129.6 %all-reduce.3.cloned.1.call-done = f32[2056,32]{0,1:T(8,128)} async-done(((f32[2056,32]{0,1:T(8,128)}), f32[2056,32]{0,1:T(8,128)}) %all-reduce.3.cloned.1.call-update) | async-done | bytes 263184 | tf_op jit(solution)/shard_map/psum | solution.py:64
  452.8 1.7 slice.35
  454.4 1.3 fusion.49
  455.8 3.1 copy.58
  458.9 3.0 copy.57
  461.9 58.3 %reduce-scatter.4.cloned.1.call-done = bf16[256,2,768]{0,2,1:T(8,128)(2,1)} async-done(((bf16[2048,2,768]{0,2,1:T(8,128)(2,1)}), bf16[256,2,768]{0,2,1:T(8,128)(2,1)}) %reduce-scatter.4.cloned.1.call-update) | async-done | bytes 786448 | tf_op jit(solution)/shard_map/reduce_scatter | solution.py:72
  520.2 3.0 copy.56
  523.3 0.0 copy-done.1
  (26 shorter events, 0.1 us)
Async XLA Ops:
  8.0 104.2 %copy-start = (bf16[2048,32]{0,1:T(8,128)(2,1)S(1)}, bf16[2048,32]{0,1:T(8,128)(2,1)}, u32[]{:S(2)}) copy-start(bf16[2048,32]{0,1:T(8,128)(2,1)} %param.15) | copy-start | bytes 393220
  13.8 71.2 %copy-start.2 = (bf16[1280,2048]{1,0:T(8,128)(2,1)}, bf16[1280,2048]{1,0:T(8,128)(2,1)S(1)}, u32[]{:S(2)}) copy-start(bf16[1280,2048]{1,0:T(8,128)(2,1)S(1)} %convolution_convert_fusion) | copy-start | bytes 15728644
  13.8 71.2 %copy-start.7 = (bf16[2048,2,768]{2,1,0:T(2,128)(2,1)S(1)}, bf16[2048,2,768]{2,1,0:T(2,128)(2,1)}, u32[]{:S(2)}) copy-start(bf16[2048,2,768]{2,1,0:T(2,128)(2,1)} %param.17) | copy-start | bytes 18874372
  13.8 75.6 %slice-start = ((s8[6291456]{0:T(1024)(128)(4,1)}), s8[4194304]{0:T(1024)(128)(4,1)S(1)}, s32[]{:S(2)}) async-start(s8[6291456]{0:T(1024)(128)(4,1)} %bitcast.77), calls=%async_computation.10 | async-start | bytes 8388608
  85.0 4.4 copy-start.3
  85.0 4.4 slice-start.1
  89.4 6.6 %copy-start.8 = (f32[2,16,40,768]{3,2,1,0:T(8,128)}, f32[2,16,40,768]{3,2,1,0:T(8,128)S(1)}, u32[]{:S(2)}) copy-start(f32[2,16,40,768]{3,2,1,0:T(8,128)S(1)} %fusion.5) | copy-start | bytes 11796484
  106.4 75.0 %all-to-all-start.1 = ((bf16[2,16,40,2048]{3,2,0,1:T(8,128)(2,1)}), bf16[2,16,40,2048]{3,2,0,1:T(8,128)(2,1)}, u32[]{:S(2)}, u32[]{:S(2)}) async-start(bf16[2,16,40,2048]{3,2,0,1:T(8,128)(2,1)} %copy.51), calls=%async_computation.1 | async-start | bytes 10485760 | tf_op jit(solution)/shard_map/all_to_all | solution.py:35
  112.1 69.3 %copy-start.4 = (bf16[512,2048]{1,0:T(8,128)(2,1)S(1)}, bf16[512,2048]{1,0:T(8,128)(2,1)}, u32[]{:S(2)}) copy-start(bf16[512,2048]{1,0:T(8,128)(2,1)} %param.11) | copy-start | bytes 6291460
  181.5 6.5 %copy-start.5 = (s32[512]{0:T(512)S(1)}, s32[512]{0:T(512)}, u32[]{:S(2)}) copy-start(s32[512]{0:T(512)} %param.13) | copy-start | bytes 6148
  181.5 6.5 %copy-start.6 = (f32[22]{0:T(128)S(1)}, f32[22]{0:T(128)}, u32[]{:S(2)}) copy-start(f32[22]{0:T(128)} %param.14) | copy-start | bytes 268
  195.5 85.2 %all-to-all-start.2 = ((bf16[32,1,40,2048]{3,2,1,0:T(8,128)(2,1)}), bf16[32,1,40,2048]{3,2,1,0:T(8,128)(2,1)}, u32[]{:S(2)}, u32[]{:S(2)}) async-start(bf16[32,1,40,2048]{3,2,1,0:T(8,128)(2,1)} %bitcast.74), calls=%async_computation.2 | async-start | bytes 10485760 | tf_op jit(solution)/shard_map/all_to_all | solution.py:65
  210.2 242.6 %all-reduce.3.cloned.1.call-start = ((), (), s32[]{:S(2)}) async-start(), calls=%async_computation.6 | async-start | bytes 557056 | tf_op jit(solution)/shard_map/psum | solution.py:64
  212.2 243.5 %reduce-scatter.8.cloned.1.call-start = ((), (), s32[]{:S(2)}) async-start(), calls=%async_computation.9 | async-start | bytes 7077888 | tf_op jit(solution)/shard_map/reduce_scatter | solution.py:72
  290.5 168.3 %reduce-scatter.6.cloned.1.call-start = ((), (), s32[]{:S(2)}) async-start(), calls=%async_computation.8 | async-start | bytes 7077888 | tf_op jit(solution)/shard_map/reduce_scatter | solution.py:72
  290.8 10.1 %copy-start.9 = (f32[2,16,40,768]{3,2,1,0:T(8,128)S(1)}, f32[2,16,40,768]{3,2,1,0:T(8,128)}, u32[]{:S(2)}) copy-start(f32[2,16,40,768]{3,2,1,0:T(8,128)} %copy-done.8) | copy-start | bytes 11796484
  299.0 1.9 copy-start.10
  310.8 209.4 %reduce-scatter.4.cloned.1.call-start = ((), (), s32[]{:S(2)}) async-start(), calls=%async_computation.7 | async-start | bytes 7077888 | tf_op jit(solution)/shard_map/reduce_scatter | solution.py:72
  323.1 200.1 %copy-start.1 = (bf16[2048,32]{0,1:T(8,128)(2,1)S(1)}, bf16[2048,32]{0,1:T(8,128)(2,1)}, u32[]{:S(2)}) copy-start(bf16[2048,32]{0,1:T(8,128)(2,1)} %param.15) | copy-start | bytes 393220
Sparse Core Ops, SparseCore 0:
  216.3 236.3 all-reduce.2
Sparse Core Ops, SparseCore 1:
  290.6 81.2 reduce-scatter.7
  374.2 71.8 reduce-scatter.5
  448.3 71.9 reduce-scatter.3
